TPU v7x, 256 devices: a whole 4x4x8 slice. The times are simulated.
256 devices in a mesh: row: 16 (over z_hi, y, core), col: 16 (over z_lo, x).
Axes of the slice: x: 4, y: 4, z: 8 (z_hi: 2, z_lo: 4; z = z_hi * 4 + z_lo), core: 2. Of those that a mesh axis runs over, the one named last changes fastest.
Arguments:
- features: bfloat16 [65536, 128], P(('col', 'row')), may hold values from -6 to 6
- weight: bfloat16 [128, 128], replicated, may hold values from -0.5 to 0.5
- tiles: bfloat16 [16, 16, 352, 128, 128], P('row', 'col'), may hold values from -0.0546875 to 0.0546875
- tile_slots: int32 [16, 16, 352], P('row', 'col'), may hold values from 0 to 1023, as said below
- tile_counts: int32 [16, 16], P('row', 'col'), may hold values from 44 to 352, as said below
- cotangent: bfloat16 [65536, 128], P(('row', 'col')), may hold values from -6 to 6
Outputs:
- hidden: bfloat16 [65536, 128], P(('row', 'col'))
- feature_grad: bfloat16 [65536, 128], P(('col', 'row'))
- weight_grad: float32 [128, 128], replicated
Inputs may be any that keep to these rules, and one draw needn't show every extreme that they name: `tile_slots`: the slots of one block are distinct. `tile_counts`: some block has all 352 slots live.
All inputs are finite; a program needn't handle non-finite values.
Results may differ from a plain program's by a relative error of at most 0.006.
Values may be sent and summed in bfloat16 or wider, within the bound.
A program may use at most 128 MiB of HBM per device.

v0:
```python
import math
import jax
import jax.numpy as jnp
from jax import lax
from jax.sharding import PartitionSpec as P


def silu_grad(values):
    sig = jax.nn.sigmoid(values)
    return sig * (1.0 + values * (1.0 - sig))


def body(features, weight, tiles, tile_slots, tile_counts, cotangent):
    tile_vals = tiles[0, 0]
    slot_ids = tile_slots[0, 0]
    live_count = tile_counts[0, 0]
    tile_size = tile_vals.shape[-1]
    share_rows = features.shape[0]
    width = features.shape[1]
    slot_total = slot_ids.shape[0]
    row_count = lax.axis_size("row")
    col_count = lax.axis_size("col")
    tile_rows = share_rows * col_count // tile_size
    tile_cols = share_rows * row_count // tile_size
    col_index = lax.axis_index("col")
    projected = jnp.dot(features, weight, preferred_element_type=jnp.float32).astype(jnp.bfloat16)
    proj_block = lax.all_gather(projected, "row", axis=0, tiled=True)
    is_live = jnp.arange(slot_total, dtype=jnp.int32) < live_count
    gathered = proj_block.reshape(tile_cols, tile_size, width)[slot_ids % tile_cols]
    products = jnp.einsum("tij,tjf->tif", tile_vals, gathered, preferred_element_type=jnp.float32)
    fwd_targets = jnp.where(is_live, slot_ids // tile_cols, tile_rows)
    partial_value = jax.ops.segment_sum(products, fwd_targets, tile_rows + 1)[:tile_rows].reshape(
        tile_rows * tile_size, width
    )
    summed = lax.psum(partial_value, "col")
    own_rows = lax.dynamic_slice_in_dim(summed, col_index * share_rows, share_rows, 0)
    hidden = jax.nn.silu(own_rows).astype(jnp.bfloat16)
    cot_block = lax.all_gather(cotangent, "col", axis=0, tiled=True)
    grad_block = (cot_block.astype(jnp.float32) * silu_grad(summed)).astype(jnp.bfloat16)
    grad_tiles = grad_block.reshape(tile_rows, tile_size, width)[slot_ids // tile_cols]
    back_products = jnp.einsum(
        "tji,tjf->tif", tile_vals, grad_tiles, preferred_element_type=jnp.float32
    )
    back_targets = jnp.where(is_live, slot_ids % tile_cols, tile_cols)
    back_partial = jax.ops.segment_sum(back_products, back_targets, tile_cols + 1)[
        :tile_cols
    ].reshape(tile_cols * tile_size, width)
    grad_proj = lax.psum_scatter(back_partial, "row", scatter_dimension=0, tiled=True).astype(
        jnp.bfloat16
    )
    feature_grad = jnp.dot(grad_proj, weight.T, preferred_element_type=jnp.float32).astype(
        jnp.bfloat16
    )
    weight_term = jnp.dot(features.T, grad_proj, preferred_element_type=jnp.float32)
    node_total = share_rows * row_count * col_count
    weight_grad = lax.psum(weight_term, ("row", "col")) / math.sqrt(node_total)
    return (hidden, feature_grad, weight_grad)


def solution(mesh):
    placed = (
        P(("col", "row"), None),
        P(),
        P("row", "col", None, None, None),
        P("row", "col", None),
        P("row", "col"),
        P(("row", "col"), None),
    )
    return jax.shard_map(
        body,
        mesh=mesh,
        in_specs=placed,
        out_specs=(P(("row", "col"), None), P(("col", "row"), None), P()),
        check_vma=False,
    )
```

profile of v0, /device:TPU:1, one launch (start us, length us, event | category | flops | bytes accessed | tf_op | source)
XLA Modules:
  0.0 771.6 jit_solution(9133756063964806921)
XLA Ops:
  7.2 0.0 all-gather.3.cloned.1.call-start
  7.2 0.8 copy-done
  8.0 1.5 convolution_convert_fusion.1
  9.6 0.0 all-gather.5.cloned.1.call-start
  9.6 0.7 all-gather.5.cloned.1.call-update
  10.3 0.0 all-reduce.3.cloned.1.call-start
  11.0 0.7 fusion.15
  11.7 0.7 fusion.13
  12.4 58.8 %all-gather.3.cloned.1.call-done = bf16[4096,128]{1,0:T(8,128)(2,1)} async-done(((bf16[256,128]{1,0:T(8,128)(2,1)}), bf16[4096,128]{1,0:T(8,128)(2,1)}) %all-gather.3.cloned.1.call-update) | async-done | bytes 1048592 | tf_op jit(solution)/shard_map/all_gather | solution.py:27
  71.3 12.2 %gather_fusion = bf16[352,128,128]{2,1,0:T(8,128)(2,1)} fusion(bf16[32,128,128]{2,1,0:T(8,128)(2,1)} %bitcast.41, s32[1024]{0:T(1024)S(1)} %pad_clamp_fusion.1), kind=kCustom, calls=%fused_computation | custom fusion | bytes 23070080 | tf_op jit(solution)/shard_map/gather | solution.py:29
  83.5 20.6 %fusion.4 = f32[352,128,128]{1,2,0:T(8,128)} fusion(bf16[352,128,128]{2,1,0:T(8,128)(2,1)} %gather_fusion, bf16[1,1,352,128,128]{4,3,2,1,0:T(8,128)(2,1)} %param.8), kind=kOutput, calls=%fused_computation.8 | convolution fusion | flops 1476395008 | bytes 46137344 | tf_op jit(solution)/shard_map/tij,tjf->tif/dot_general | solution.py:30
  104.1 23.5 %copy.13 = f32[352,128,128]{2,1,0:T(8,128)} copy(f32[352,128,128]{1,2,0:T(8,128)} %fusion.4) | data formatting | bytes 46137344 | tf_op jit(solution)/shard_map/tij,tjf->tif/dot_general | solution.py:30
  127.6 0.2 broadcast.191.clone
  127.8 46.0 %scatter_fusion = f32[33,128,128]{2,1,0:T(8,128)S(1)} fusion(f32[33,128,128]{2,1,0:T(8,128)S(1)} %broadcast.191.clone, s32[352]{0:T(512)S(1)} %get-tuple-element.10, f32[352,128,128]{2,1,0:T(8,128)} %copy.13), kind=kCustom, calls=%fused_computation.2 | custom fusion | flops 5767168 | bytes 69207424 | tf_op jit(solution)/shard_map/scatter-add | solution.py:32
  173.9 1.5 slice.12
  175.4 0.2 reduce-scatter.2.cloned.1.call-start
  175.7 153.0 %all-reduce.3.cloned.1.call-done = f32[4096,128]{1,0:T(8,128)} async-done(((f32[4096,128]{1,0:T(8,128)}), f32[4096,128]{1,0:T(8,128)}) %all-reduce.3.cloned.1.call-update) | async-done | bytes 2097168 | tf_op jit(solution)/shard_map/psum | solution.py:35
  328.6 2.6 multiply_convert_fusion
  331.3 11.0 %gather_fusion.1 = bf16[352,128,128]{2,1,0:T(8,128)(2,1)} fusion(bf16[32,128,128]{2,1,0:T(8,128)(2,1)S(1)} %bitcast.40, s32[1024]{0:T(1024)S(1)} %pad_clamp_fusion), kind=kCustom, calls=%fused_computation.1 | custom fusion | bytes 23070080 | tf_op jit(solution)/shard_map/gather | solution.py:40
  342.3 14.4 %fusion.7 = f32[352,128,128]{1,2,0:T(8,128)} fusion(bf16[352,128,128]{2,1,0:T(8,128)(2,1)} %gather_fusion.1, bf16[1,1,352,128,128]{4,3,2,1,0:T(8,128)(2,1)} %param.8), kind=kOutput, calls=%fused_computation.9 | convolution fusion | flops 1476395008 | bytes 46137344 | tf_op jit(solution)/shard_map/tji,tjf->tif/dot_general | solution.py:41
  356.7 23.5 %copy.15 = f32[352,128,128]{2,1,0:T(8,128)} copy(f32[352,128,128]{1,2,0:T(8,128)} %fusion.7) | data formatting | bytes 46137344 | tf_op jit(solution)/shard_map/tji,tjf->tif/dot_general | solution.py:41
  380.2 0.2 broadcast.191
  380.4 46.0 %scatter_fusion.1 = f32[33,128,128]{2,1,0:T(8,128)S(1)} fusion(f32[33,128,128]{2,1,0:T(8,128)S(1)} %broadcast.191, s32[352]{0:T(512)S(1)} %get-tuple-element.11, f32[352,128,128]{2,1,0:T(8,128)} %copy.15), kind=kCustom, calls=%fused_computation.3 | custom fusion | flops 5767168 | bytes 69207424 | tf_op jit(solution)/shard_map/scatter-add | solution.py:45
  426.4 1.5 slice.13
  428.0 0.0 all-reduce.5.cloned.1.call-start
  428.0 1.6 multiply_convert_fusion.1
  429.6 92.6 %reduce-scatter.2.cloned.1.call-done = f32[256,128]{1,0:T(8,128)} async-done(((f32[4096,128]{1,0:T(8,128)}), f32[256,128]{1,0:T(8,128)}) %reduce-scatter.2.cloned.1.call-update) | async-done | bytes 131088 | tf_op jit(solution)/shard_map/reduce_scatter | solution.py:48
  522.2 1.7 convolution_bitcast_fusion
  524.0 1.7 convolution_convert_fusion
  525.7 237.9 %all-reduce.5.cloned.1.call-done = f32[128,128]{0,1:T(8,128)} async-done(((f32[128,128]{0,1:T(8,128)}), f32[128,128]{0,1:T(8,128)}) %all-reduce.5.cloned.1.call-update) | async-done | bytes 65552 | tf_op jit(solution)/shard_map/psum | solution.py:56
  763.5 0.8 broadcast_multiply_fusion
  764.4 0.7 copy.16
  (10 shorter events, 0.1 us)
Async XLA Ops:
  7.2 0.8 copy-start
  7.2 64.1 %all-gather.3.cloned.1.call-start = ((), (), s32[]{:S(2)}) async-start(), calls=%async_computation.1 | async-start | bytes 1114112 | tf_op jit(solution)/shard_map/all_gather | solution.py:27
  9.6 166.1 %all-gather.5.cloned.1.call-start = ((), (), s32[]{:S(2)}) async-start(), calls=%async_computation.3 | async-start | bytes 1114112 | tf_op jit(solution)/shard_map/all_gather | solution.py:38
  10.3 318.3 %all-reduce.3.cloned.1.call-start = ((), (), s32[]{:S(2)}) async-start(), calls=%async_computation.2 | async-start | bytes 4194304 | tf_op jit(solution)/shard_map/psum | solution.py:35
  175.4 346.8 %reduce-scatter.2.cloned.1.call-start = ((), (), s32[]{:S(2)}) async-start(), calls=%async_computation.4 | async-start | bytes 2228224 | tf_op jit(solution)/shard_map/reduce_scatter | solution.py:48
  380.4 143.5 %copy-start.1 = (bf16[128,128]{1,0:T(8,128)(2,1)S(1)}, bf16[128,128]{1,0:T(8,128)(2,1)}, u32[]{:S(2)}) copy-start(bf16[128,128]{1,0:T(8,128)(2,1)} %param.7) | copy-start | bytes 98308
  428.0 335.5 %all-reduce.5.cloned.1.call-start = ((), (), s32[]{:S(2)}) async-start(), calls=%async_computation.5 | async-start | bytes 131072 | tf_op jit(solution)/shard_map/psum | solution.py:56
Sparse Core Ops, SparseCore 0:
  11.3 59.9 all-gather.2
  73.1 65.9 all-gather.4
  175.5 153.0 all-reduce.2
  428.1 94.0 reduce-scatter.1
  528.1 235.3 all-reduce.4
where the time goes:
time: 774 us; the launch traced here: 772 us
  waiting for transfers between devices  543 us (70%)
  other arithmetic  98.5 us (13%)
  local copies, waits for them, and re-layouts  75.1 us (10%)
  matrix products  40 us (5%)
  between operations  14.5 us (2%)
    psum x1, waiting for transfers between devices, body(): weight_grad = lax.psum(weight_term, ('row', 'col')) / math.sqrt(node_total)  238 us
    psum x1, waiting for transfers between devices, body(): summed = lax.psum(partial_value, 'col')  153 us
    reduce_scatter x1, waiting for transfers between devices, body(): lax.psum_scatter(back_partial, 'row', scatter_dimension=0, tiled=True)  92.6 us
    all_gather x1, waiting for transfers between devices, body(): proj_block = lax.all_gather(projected, 'row', axis=0, tiled=True)  58.8 us
    scatter-add x1, other arithmetic, body(): jax.ops.segment_sum(products, fwd_targets, tile_rows + 1)[:tile_rows]  46 us
    scatter-add x1, other arithmetic, body(): jax.ops.segment_sum(back_products, back_targets, tile_cols + 1)[:tile_cols]  46 us
    dot_general x1, local copies, waits for them, and re-layouts, body(): jnp.einsum('tij,tjf->tif', tile_vals, gathered, preferred_element_type=jn...  23.5 us
    dot_general x1, local copies, waits for them, and re-layouts, body(): jnp.einsum('tji,tjf->tif', tile_vals, grad_tiles, preferred_element_type=...  23.5 us
  transfers between devices with their start and end apart: 5, of which 4 were waited for; matrix products, arithmetic and copies ran while one was open for 14% of the time, Pallas kernels for 0%

commit v1 on v0

--- a/solution.py
+++ b/solution.py
@@ -32,7 +32,7 @@
     partial_value = jax.ops.segment_sum(products, fwd_targets, tile_rows + 1)[:tile_rows].reshape(
         tile_rows * tile_size, width
     )
-    summed = lax.psum(partial_value, "col")
+    summed = jnp.sum(lax.all_gather(partial_value, "col"), axis=0)
     own_rows = lax.dynamic_slice_in_dim(summed, col_index * share_rows, share_rows, 0)
     hidden = jax.nn.silu(own_rows).astype(jnp.bfloat16)
     cot_block = lax.all_gather(cotangent, "col", axis=0, tiled=True)

time: 774 us -> 1040 us (1.34)
  waiting for transfers between devices: 543 us -> 799 us
  other arithmetic: 98.5 us -> 110 us
    all_gather x0 -> x1, waiting for transfers between devices: none -> 350 us  [body(): summed = jnp.sum(lax.all_gather(partial_value, 'col'), axis=0)]
    psum x1 -> x0, waiting for transfers between devices: 153 us -> none  [body(): summed = lax.psum(partial_value, 'col')]
    all_gather x1, waiting for transfers between devices: 0.02 us -> 57.6 us  [body(): cot_block = lax.all_gather(cotangent, 'col', axis=0, tiled=True)]
    reduce_sum x0 -> x1, other arithmetic: none -> 11.8 us  [body(): summed = jnp.sum(lax.all_gather(partial_value, 'col'), axis=0)]
  transfers between devices with their start and end apart: 5 -> 5, of which waited for: 4 -> 5; matrix products, arithmetic and copies ran while one was open for 14% -> 2% of each run, Pallas kernels for 0% -> 0%
where the time goes in v1:
time: 1040 us
  waiting for transfers between devices  799 us (77%)
  other arithmetic  110 us (11%)
  local copies, waits for them, and re-layouts  75.1 us (7%)
  matrix products  40 us (4%)
  between operations  14.5 us (1%)
    all_gather x1, waiting for transfers between devices, body(): summed = jnp.sum(lax.all_gather(partial_value, 'col'), axis=0)  350 us
    psum x1, waiting for transfers between devices, body(): weight_grad = lax.psum(weight_term, ('row', 'col')) / math.sqrt(node_total)  238 us
    reduce_scatter x1, waiting for transfers between devices, body(): lax.psum_scatter(back_partial, 'row', scatter_dimension=0, tiled=True)  93.2 us
    all_gather x1, waiting for transfers between devices, body(): proj_block = lax.all_gather(projected, 'row', axis=0, tiled=True)  59.6 us
    all_gather x1, waiting for transfers between devices, body(): cot_block = lax.all_gather(cotangent, 'col', axis=0, tiled=True)  57.6 us
    scatter-add x1, other arithmetic, body(): jax.ops.segment_sum(products, fwd_targets, tile_rows + 1)[:tile_rows]  46 us
    scatter-add x1, other arithmetic, body(): jax.ops.segment_sum(back_products, back_targets, tile_cols + 1)[:tile_cols]  46 us
    dot_general x1, local copies, waits for them, and re-layouts, body(): jnp.einsum('tji,tjf->tif', tile_vals, grad_tiles, preferred_element_type=...  23.5 us
  transfers between devices with their start and end apart: 5, of which 5 were waited for; matrix products, arithmetic and copies ran while one was open for 2% of the time, Pallas kernels for 0%

profile of v1, /device:TPU:1, one launch (start us, length us, event | category | flops | bytes accessed | tf_op | source)
XLA Modules:
  0.0 1038.2 jit_solution(16585602846013943177)
XLA Ops:
  7.2 0.8 copy-done
  8.0 1.5 convolution_convert_fusion.1
  9.6 0.0 all-gather.6.cloned.1.call-start
  10.3 0.7 fusion.15
  11.0 0.7 fusion.13
  11.7 59.6 %all-gather.4.cloned.1.call-done = bf16[4096,128]{1,0:T(8,128)(2,1)} async-done(((bf16[256,128]{1,0:T(8,128)(2,1)}), bf16[4096,128]{1,0:T(8,128)(2,1)}) %all-gather.4.cloned.1.call-update) | async-done | bytes 1048592 | tf_op jit(solution)/shard_map/all_gather | solution.py:27
  71.3 12.2 %gather_fusion = bf16[352,128,128]{2,1,0:T(8,128)(2,1)} fusion(bf16[32,128,128]{2,1,0:T(8,128)(2,1)} %bitcast.41, s32[1024]{0:T(1024)S(1)} %pad_clamp_fusion.1), kind=kCustom, calls=%fused_computation | custom fusion | bytes 23070080 | tf_op jit(solution)/shard_map/gather | solution.py:29
  83.5 20.6 %fusion.4 = f32[352,128,128]{1,2,0:T(8,128)} fusion(bf16[352,128,128]{2,1,0:T(8,128)(2,1)} %gather_fusion, bf16[1,1,352,128,128]{4,3,2,1,0:T(8,128)(2,1)} %param.8), kind=kOutput, calls=%fused_computation.8 | convolution fusion | flops 1476395008 | bytes 46137344 | tf_op jit(solution)/shard_map/tij,tjf->tif/dot_general | solution.py:30
  104.1 23.5 %copy.18 = f32[352,128,128]{2,1,0:T(8,128)} copy(f32[352,128,128]{1,2,0:T(8,128)} %fusion.4) | data formatting | bytes 46137344 | tf_op jit(solution)/shard_map/tij,tjf->tif/dot_general | solution.py:30
  127.5 0.2 broadcast.191.clone
  127.8 46.0 %scatter_fusion = f32[33,128,128]{2,1,0:T(8,128)S(1)} fusion(f32[33,128,128]{2,1,0:T(8,128)S(1)} %broadcast.191.clone, s32[352]{0:T(512)S(1)} %get-tuple-element.13, f32[352,128,128]{2,1,0:T(8,128)} %copy.18), kind=kCustom, calls=%fused_computation.2 | custom fusion | flops 5767168 | bytes 69207424 | tf_op jit(solution)/shard_map/scatter-add | solution.py:32
  173.8 1.5 slice.12
  175.3 0.7 all-gather.8.cloned.1.call-update
  176.0 0.2 reduce-scatter.2.cloned.1.call-start
  176.3 349.5 %all-gather.6.cloned.1.call-done = f32[16,4096,128]{2,1,0:T(8,128)} async-done(((f32[1,4096,128]{2,1,0:T(8,128)}), f32[16,4096,128]{2,1,0:T(8,128)}) %all-gather.6.cloned.1.call-update) | async-done | bytes 33554448 | tf_op jit(solution)/shard_map/all_gather | solution.py:35
  525.8 11.8 %reduce_sum.9 = f32[4096,128]{1,0:T(8,128)S(1)} reduce(f32[16,4096,128]{2,1,0:T(8,128)} %all-gather.6.cloned.1.call-done, f32[]{:T(128)} %constant.42.clone.1), dimensions={0}, to_apply=%region_1.2 | reduce | flops 7864320 | bytes 35651588 | tf_op jit(solution)/shard_map/reduce_sum | solution.py:35
  537.6 57.6 %all-gather.8.cloned.1.call-done = bf16[4096,128]{1,0:T(8,128)(2,1)} async-done(((bf16[256,128]{1,0:T(8,128)(2,1)}), bf16[4096,128]{1,0:T(8,128)(2,1)}) %all-gather.8.cloned.1.call-update) | async-done | bytes 1048592 | tf_op jit(solution)/shard_map/all_gather | solution.py:38
  595.2 2.0 multiply_convert_fusion
  597.2 11.0 %gather_fusion.1 = bf16[352,128,128]{2,1,0:T(8,128)(2,1)} fusion(bf16[32,128,128]{2,1,0:T(8,128)(2,1)S(1)} %bitcast.40, s32[1024]{0:T(1024)S(1)} %pad_clamp_fusion), kind=kCustom, calls=%fused_computation.1 | custom fusion | bytes 23070080 | tf_op jit(solution)/shard_map/gather | solution.py:40
  608.2 14.4 %fusion.7 = f32[352,128,128]{1,2,0:T(8,128)} fusion(bf16[352,128,128]{2,1,0:T(8,128)(2,1)} %gather_fusion.1, bf16[1,1,352,128,128]{4,3,2,1,0:T(8,128)(2,1)} %param.8), kind=kOutput, calls=%fused_computation.9 | convolution fusion | flops 1476395008 | bytes 46137344 | tf_op jit(solution)/shard_map/tji,tjf->tif/dot_general | solution.py:41
  622.6 23.5 %copy.20 = f32[352,128,128]{2,1,0:T(8,128)} copy(f32[352,128,128]{1,2,0:T(8,128)} %fusion.7) | data formatting | bytes 46137344 | tf_op jit(solution)/shard_map/tji,tjf->tif/dot_general | solution.py:41
  646.1 0.2 broadcast.191
  646.3 46.0 %scatter_fusion.1 = f32[33,128,128]{2,1,0:T(8,128)S(1)} fusion(f32[33,128,128]{2,1,0:T(8,128)S(1)} %broadcast.191, s32[352]{0:T(512)S(1)} %get-tuple-element.14, f32[352,128,128]{2,1,0:T(8,128)} %copy.20), kind=kCustom, calls=%fused_computation.3 | custom fusion | flops 5767168 | bytes 69207424 | tf_op jit(solution)/shard_map/scatter-add | solution.py:45
  692.3 1.5 slice.13
  693.9 0.0 all-reduce.2.cloned.1.call-start
  693.9 1.6 multiply_convert_fusion.1
  695.5 93.2 %reduce-scatter.2.cloned.1.call-done = f32[256,128]{1,0:T(8,128)} async-done(((f32[4096,128]{1,0:T(8,128)}), f32[256,128]{1,0:T(8,128)}) %reduce-scatter.2.cloned.1.call-update) | async-done | bytes 131088 | tf_op jit(solution)/shard_map/reduce_scatter | solution.py:48
  788.7 1.7 convolution_bitcast_fusion
  790.5 1.7 convolution_convert_fusion
  792.2 238.0 %all-reduce.2.cloned.1.call-done = f32[128,128]{0,1:T(8,128)} async-done(((f32[128,128]{0,1:T(8,128)}), f32[128,128]{0,1:T(8,128)}) %all-reduce.2.cloned.1.call-update) | async-done | bytes 65552 | tf_op jit(solution)/shard_map/psum | solution.py:56
  1030.1 0.8 broadcast_multiply_fusion
  1031.0 0.7 copy.21
  (13 shorter events, 0.2 us)
Async XLA Ops:
  7.2 0.8 copy-start
  7.2 64.1 %all-gather.4.cloned.1.call-start = ((), (), s32[]{:S(2)}) async-start(), calls=%async_computation.1 | async-start | bytes 1114112 | tf_op jit(solution)/shard_map/all_gather | solution.py:27
  9.6 516.2 %all-gather.6.cloned.1.call-start = ((), (), s32[]{:S(2)}) async-start(), calls=%async_computation.2 | async-start | bytes 35651584 | tf_op jit(solution)/shard_map/all_gather | solution.py:35
  175.3 419.9 %all-gather.8.cloned.1.call-start = ((), (), s32[]{:S(2)}) async-start(), calls=%async_computation.3 | async-start | bytes 1114112 | tf_op jit(solution)/shard_map/all_gather | solution.py:38
  176.0 612.7 %reduce-scatter.2.cloned.1.call-start = ((), (), s32[]{:S(2)}) async-start(), calls=%async_computation.4 | async-start | bytes 2228224 | tf_op jit(solution)/shard_map/reduce_scatter | solution.py:48
  537.6 70.6 %copy-start.1 = (f32[4096,128]{1,0:T(8,128)}, f32[4096,128]{1,0:T(8,128)S(1)}, u32[]{:S(2)}) copy-start(f32[4096,128]{1,0:T(8,128)S(1)} %reduce_sum.9) | copy-start | bytes 6291460
  646.3 144.1 %copy-start.2 = (bf16[128,128]{1,0:T(8,128)(2,1)S(1)}, bf16[128,128]{1,0:T(8,128)(2,1)}, u32[]{:S(2)}) copy-start(bf16[128,128]{1,0:T(8,128)(2,1)} %param.7) | copy-start | bytes 98308
  693.9 336.3 %all-reduce.2.cloned.1.call-start = ((), (), s32[]{:S(2)}) async-start(), calls=%async_computation.5 | async-start | bytes 131072 | tf_op jit(solution)/shard_map/psum | solution.py:56
Sparse Core Ops, SparseCore 0:
  11.3 59.9 all-gather.3
  175.4 350.3 all-gather.5
  527.6 67.5 all-gather.7
  694.0 94.6 reduce-scatter.1
  794.6 235.4 all-reduce.1
